TPU v7x, 32 devices: a whole 2x2x4 slice. The times are simulated.
32 devices in a mesh: passage: 2 (over x), brick: 16 (over z, y, core).
Axes of the slice: x: 2, y: 2, z: 4, core: 2. Of those that a mesh axis runs over, the one named last changes fastest.
Arguments:
- jac_blocks: bfloat16 [2, 25, 16, 8192], P('passage', None, None, 'brick'), may hold values from -6 to 6
- psi_start: float32 [2, 10, 16, 64, 128], P('passage', None, 'brick'), may hold values from -6 to 6
- source: float32 [2, 10, 16, 64, 128], P('passage', None, 'brick'), may hold values from -6 to 6
- pseudo_step: float32 [2, 16, 64, 128], P('passage', 'brick'), may hold values from 0.1 to 0.4
- dissipation: float32 [2, 16, 64, 128], P('passage', 'brick'), may hold values from 0.04 to 0.15
- freq_volume: float32 [2, 16, 64, 128], P('passage', 'brick'), may hold values from 0.2 to 2
- normals: float32 [2, 3, 16, 64], P('passage', None, 'brick'), may hold values from -6 to 6
- face_owner: int32 [2, 1024, 1], P('passage', 'brick'), may hold values from 0 to 15; in each aligned block of 64 rows (0 to 63, 64 to 127, ..., all dimensions but the last counted through in order) at most 16 rows name the same one
- face_slot: int32 [2, 1024], P('passage', 'brick'), may hold values from 0 to 255
Outputs:
- adjoint: float32 [2, 10, 16, 64, 128], P('passage', None, 'brick')
- sensitivity: float32 [2, 6, 4096], P('passage', None, 'brick')
Inputs may be any that keep to these rules, and one draw needn't show every extreme that they name: `face_owner`: in the 64 faces of one device (aligned blocks of the rows), no brick is named by more than 16 faces, and in some block some brick is named by exactly 16.
All inputs are finite; a program needn't handle non-finite values.
Results may differ from a plain program's by a relative error of at most 0.0003.
Values may be sent and summed in bfloat16 or wider, within the bound.
A program may use at most 64 MiB of HBM per device.

v0:
```python
import functools
import math

import jax
import jax.numpy as jnp
from jax import lax
from jax.experimental import pallas as pl
from jax.experimental.pallas import tpu as pltpu
from jax.sharding import PartitionSpec as P

NODE_DEV = 256
SWEEPS = 2
ND = 1
BLADES = 36
LANES = 128
SUB = 8
CODE = 32767.0
BOUND = 6.0
MESH = pl.DeviceIdType.MESH


def kernel(
    B, passes, phase_angle,
    jac_h, psi_h, source_h, pstep_h, diss_h, freq_h, normals_h, owner_h, slot_h,
    adj_h, sens,
    jac, source, pstep, diss, freq, normals_v, owner, slot, adj, normals, ids,
    jpack, jsend, jrecv, jflat, pad0, pad1, low, high,
    code0, low0, high0, code1, low1, high1, scale1, low_scale, high_scale,
    rim_send, rim_recv, idbuf, valbuf, hits, turned, wall_send, low_wall, high_wall, rim_wall,
    l_s, o_s, j_s, j_r, h_s, h_r, c_s, c_r, w_s, w_r, r_s, r_r, i_s, i_r, v_s, v_r,
):
    me = lax.axis_index("brick")
    mp = lax.axis_index("passage")
    NJ, NK = source.shape[1], source.shape[2]
    R = jac.shape[2] // LANES
    planes = jac.shape[1]
    rows = 25 * R
    pitch = jpack.shape[0] // planes
    others = range(1, B)
    up_p = lax.rem(mp + 1, passes)
    down_p = lax.rem(mp + passes - 1, passes)

    barrier = pltpu.get_barrier_semaphore()
    for d in others:
        pl.semaphore_signal(
            barrier, inc=1, device_id={"brick": lax.rem(me + d, B)}, device_id_type=MESH
        )
    pl.semaphore_signal(barrier, inc=1, device_id={"passage": up_p}, device_id_type=MESH)
    greeted = B
    if passes > 2:
        pl.semaphore_signal(barrier, inc=1, device_id={"passage": down_p}, device_id_type=MESH)
        greeted += 1

    psi = pad0.at[:, pl.ds(SUB, NJ), :]
    loads = [
        pltpu.make_async_copy(src, dst, l_s.at[k])
        for k, (src, dst) in enumerate((
            (jac_h, jac), (psi_h, psi), (owner_h, owner), (slot_h, slot), (normals_h, normals_v),
            (source_h, source), (pstep_h, pstep), (diss_h, diss), (freq_h, freq),
        ))
    ]
    for load in loads:
        load.start()

    @pl.when(me == 0)
    def _():
        low0[...] = jnp.zeros_like(low0)
        low1[...] = jnp.zeros_like(low1)
        low_scale[...] = jnp.zeros_like(low_scale)
        low_wall[...] = jnp.zeros_like(low_wall)

    @pl.when(me == B - 1)
    def _():
        high0[...] = jnp.zeros_like(high0)
        high1[...] = jnp.zeros_like(high1)
        high_scale[...] = jnp.zeros_like(high_scale)
        high_wall[...] = jnp.zeros_like(high_wall)

    loads[0].wait()
    for n in range(25):
        for r in range(R):
            for g in range(planes // SUB):
                x = jac[n, pl.ds(g * SUB, SUB), pl.ds(r * LANES, LANES)].astype(jnp.float32)
                jpack[pl.ds(g * SUB * pitch + r * 25 + n, SUB, stride=pitch), :] = x
    for p in range(planes):
        jsend[p, :, :] = jpack[pl.ds(p * pitch, rows), :].astype(jnp.bfloat16)

    def fill_rims(sweep, field, first, last):
        for c in range(10):
            rim_send[sweep, 0, pl.ds(c, 1), :] = field[c, pl.ds(last, 1), :]
            rim_send[sweep, 1, pl.ds(c, 1), :] = field[c, pl.ds(first, 1), :]

    def rim_copies(sweep):
        return [
            pltpu.make_async_remote_copy(
                src_ref=rim_send.at[sweep, k],
                dst_ref=rim_recv.at[sweep, k],
                send_sem=r_s.at[sweep, k],
                recv_sem=r_r.at[sweep, k],
                device_id={"passage": peer},
                device_id_type=MESH,
            )
            for k, peer in ((0, up_p), (1, down_p))
        ]

    def halo_copies(h_s, h_r, sweep, src, low, high):
        up = pltpu.make_async_remote_copy(
            src_ref=src, dst_ref=low, send_sem=h_s.at[sweep, 0], recv_sem=h_r.at[sweep, 0],
            device_id={"brick": lax.rem(me + 1, B)}, device_id_type=MESH,
        )
        down = pltpu.make_async_remote_copy(
            src_ref=src, dst_ref=high, send_sem=h_s.at[sweep, 1], recv_sem=h_r.at[sweep, 1],
            device_id={"brick": lax.rem(me + B - 1, B)}, device_id_type=MESH,
        )
        return up, down

    def halo_start(up, down):
        @pl.when(me < B - 1)
        def _():
            up.start()

        @pl.when(me > 0)
        def _():
            down.start()

    def halo_recv(up, down):
        @pl.when(me > 0)
        def _():
            up.wait_recv()

        @pl.when(me < B - 1)
        def _():
            down.wait_recv()

    def halo_sent(up, down):
        @pl.when(me < B - 1)
        def _():
            up.wait_send()

        @pl.when(me > 0)
        def _():
            down.wait_send()

    loads[1].wait()
    fill_rims(0, pad0, SUB, SUB + NJ - 1)
    for c in range(10):
        q = jnp.round(pad0[c, pl.ds(SUB, NJ), :] * (CODE / BOUND))
        code0[c, :, :] = q.astype(jnp.int32).astype(jnp.int16)
    loads[2].wait()
    loads[3].wait()
    faces = owner.shape[1]
    ids[...] = jnp.full((SUB, LANES), -1, jnp.int32)
    ids[0:1, pl.ds(0, faces)] = owner[...] * NODE_DEV + slot[...]
    idbuf[pl.ds(me, 1), :, :] = ids[...].reshape(1, SUB, LANES)

    j_copies, id_copies, val_copies = [], [], []
    for k, d in enumerate(others):
        peer = lax.rem(me + d, B)
        j_copies.append(pltpu.make_async_remote_copy(
            src_ref=jsend.at[peer], dst_ref=jrecv.at[me], send_sem=j_s.at[k], recv_sem=j_r.at[k],
            device_id={"brick": peer}, device_id_type=MESH))
        id_copies.append(pltpu.make_async_remote_copy(
            src_ref=ids, dst_ref=idbuf.at[me], send_sem=i_s.at[k], recv_sem=i_r.at[k],
            device_id={"brick": peer}, device_id_type=MESH))
        val_copies.append(pltpu.make_async_remote_copy(
            src_ref=valbuf.at[me], dst_ref=valbuf.at[me], send_sem=v_s.at[k], recv_sem=v_r.at[k],
            device_id={"brick": peer}, device_id_type=MESH))
    rims0, rims1 = rim_copies(0), rim_copies(1)
    halo0 = halo_copies(h_s, h_r, 0, code0, low0, high0)
    halo1 = halo_copies(h_s, h_r, 1, code1, low1, high1)
    walls = halo_copies(w_s, w_r, 0, wall_send, low_wall, high_wall)
    scales = halo_copies(c_s, c_r, 0, scale1, low_scale, high_scale)

    pl.semaphore_wait(barrier, greeted)
    for copy in id_copies:
        copy.start()
    for copy in j_copies:
        copy.start()
    for copy in rims0:
        copy.start()
    halo_start(*halo0)

    jrecv[pl.ds(me, 1), :, :] = jsend[pl.ds(me, 1), :, :]
    for load in loads[4:]:
        load.wait()
    normals[...] = jnp.zeros_like(normals)
    for d in range(3):
        for k in (d, 3 + d):
            normals[pl.ds(k, 1), pl.ds(0, faces)] = normals_v[d, :, :]

    lane = lax.broadcasted_iota(jnp.int32, (SUB, NK), 1)

    def place_rims(sweep, pad):
        for k, (edge, turn, row) in enumerate(
            ((0, -phase_angle, SUB - 1), (passes - 1, phase_angle, SUB + NJ))
        ):
            rim = rim_recv[sweep, k, :, :]
            re, im = rim[0:5], rim[5:10]
            at_edge = mp == edge
            cosine = jnp.where(at_edge, math.cos(turn), 1.0).astype(jnp.float32)
            sine = jnp.where(at_edge, math.sin(turn), 0.0).astype(jnp.float32)
            re, im = re * cosine - im * sine, re * sine + im * cosine
            if sweep == SWEEPS - 1:
                rim_wall[k, 0:5, :] = re
                rim_wall[k, SUB : SUB + 5, :] = im
            for c in range(5):
                pad[c, pl.ds(row, 1), :] = re[c : c + 1]
                pad[5 + c, pl.ds(row, 1), :] = im[c : c + 1]

    def advance(pad, low, high, out, shift):
        for t in range(NJ // SUB):
            at = pl.ds(t * SUB, SUB)
            om, ds_, ps = freq[at, :], diss[at, :], pstep[at, :]
            us, lows, highs = [], [], []
            for c in range(10):
                us.append(pad[c, pl.ds(SUB + t * SUB, SUB), :])
                lows.append(low[c, at, :])
                highs.append(high[c, at, :])
            diff = [0.5 * (h - l) for h, l in zip(highs, lows)]
            conv = [None] * 10
            for n in range(5):
                for m in range(5):
                    tile = jflat[pl.ds(t * SUB * 25 + n * 5 + m, SUB, stride=25), :]
                    for part in (0, 5):
                        term = tile * diff[part + n]
                        conv[part + m] = term if conv[part + m] is None else conv[part + m] + term
            for c in range(10):
                u = us[c]
                beside = highs[c] + lows[c]
                beside = beside + pad[c, pl.ds(SUB + t * SUB + 1, SUB), :]
                beside = beside + pad[c, pl.ds(SUB + t * SUB - 1, SUB), :]
                beside = beside + jnp.where(lane == NK - 1, 0.0, pltpu.roll(u, NK - 1, 1))
                beside = beside + jnp.where(lane == 0, 0.0, pltpu.roll(u, 1, 1))
                spin = om * us[c + 5] if c < 5 else -(om * us[c - 5])
                resid = conv[c] + spin + ds_ * (6.0 * u - beside) - source[c, at, :]
                out[c, pl.ds(shift + t * SUB, SUB), :] = u - ps * resid

    lanes = lax.broadcasted_iota(jnp.int32, (NJ, NK), 1)

    def turn_over(slot, pieces):
        packed = jnp.zeros((NJ, NK), jnp.float32)
        for to, column, x in pieces:
            shift = (to - column) % NK
            x = pltpu.roll(x, shift, 1) if shift else x
            packed = jnp.where(lanes == to, x, packed)
        if NJ < LANES:
            packed = jnp.concatenate([packed, jnp.zeros((LANES - NJ, NK), jnp.float32)], axis=0)
        turned[slot, :, :] = packed.T

    turn_over(0, [(0, 0, pstep[...]), (1, 0, diss[...]), (2, 0, freq[...])]
              + [(SUB + c + c // 5 * 3, 0, source[c, :, :]) for c in range(10)])
    for copy in id_copies:
        copy.wait_recv()
    node = lax.broadcasted_iota(jnp.int32, (NODE_DEV, LANES), 0) + me * NODE_DEV
    for s in range(B):
        hits[s, :, :] = jnp.where(idbuf[s, 0:1, :] == node, 1.0, 0.0).astype(jnp.bfloat16)

    for copy in rims0:
        copy.wait_recv()
    place_rims(0, pad0)
    halo_recv(*halo0)
    for code, field in ((low0, low), (high0, high)):
        for c in range(10):
            field[c, :, :] = code[c, :, :].astype(jnp.int32).astype(jnp.float32) * (BOUND / CODE)
    for copy in j_copies:
        copy.wait_recv()
    for s in range(B):
        jflat[pl.ds(s * rows, rows), :] = jrecv[s, :, :].astype(jnp.float32)

    advance(pad0, low, high, pad1, SUB)
    fill_rims(1, pad1, SUB, SUB + NJ - 1)
    for copy in rims1:
        copy.start()
    turn_over(2, [
        (16 * k + c + c // 5 * 3, k, pad1[c, pl.ds(SUB, NJ), :]) for k in range(2) for c in range(10)
    ])
    wall_send[...] = turned[2, 0:16, :]
    halo_start(*walls)
    for c in range(10):
        x = pad1[c, pl.ds(SUB, NJ), :]
        top = jnp.maximum(jnp.max(jnp.abs(x), axis=0, keepdims=True), 1e-30)
        scale1[pl.ds(c, 1), :] = top * (1.0 / CODE)
        code1[c, :, :] = jnp.round(x * (CODE / top)).astype(jnp.int32).astype(jnp.int16)
    halo_start(*scales)
    halo_start(*halo1)
    for copy in rims1:
        copy.wait_recv()
    place_rims(1, pad1)
    turn_over(1, [
        (SUB * n + m, 0, jflat[pl.ds(n * 5 + m, NJ, stride=25), :])
        for n in range(5) for m in range(5)
    ])
    halo_recv(*walls)
    face = lax.broadcasted_iota(jnp.int32, (5, LANES), 1)
    sides = normals[0:3, :]
    valbuf[pl.ds(me, 1), :, :] = jnp.zeros((1, SUB, LANES), jnp.float32)
    for part in range(2):
        at = pl.ds(SUB * part, 5)
        u, lo, hi = turned[2, at, :], low_wall[at, :], high_wall[at, :]
        diff = 0.5 * (hi - lo)
        conv = turned[1, 0:5, :] * diff[0:1]
        for n in range(1, 5):
            conv = conv + turned[1, pl.ds(SUB * n, 5), :] * diff[n : n + 1]
        below = jnp.where(face == 0, rim_wall[0, at, :][:, 0:1], pltpu.roll(u, 1, 1))
        above = jnp.where(face == NJ - 1, rim_wall[1, at, :][:, 0:1], pltpu.roll(u, LANES - 1, 1))
        beside = hi + lo + above + below + turned[2, pl.ds(16 + SUB * part, 5), :]
        spin = turned[0, 2:3, :] * turned[2, pl.ds(SUB * (1 - part), 5), :]
        spin = -spin if part else spin
        resid = conv + spin + turned[0, 1:2, :] * (6.0 * u - beside)
        resid = resid - turned[0, pl.ds(SUB + SUB * part, 5), :]
        fresh = u - turned[0, 0:1, :] * resid
        valbuf[pl.ds(me, 1), pl.ds(3 * part, 3), :] = (fresh[1:4] * sides)[None]
    for copy in val_copies:
        copy.start()

    halo_recv(*scales)
    halo_recv(*halo1)
    for code, scale, field in ((low1, low_scale, low), (high1, high_scale, high)):
        for c in range(10):
            f = code[c, :, :].astype(jnp.int32).astype(jnp.float32)
            field[c, :, :] = f * scale[pl.ds(c, 1), :]
    advance(pad1, low, high, adj, 0)
    store = pltpu.make_async_copy(adj, adj_h, o_s)

    store.start()

    for copy in val_copies:
        copy.wait_recv()
    total = jnp.zeros((3 * SUB, NODE_DEV), jnp.float32)
    for s in range(B):
        v = valbuf[s, :, :]
        a = v.astype(jnp.bfloat16).astype(jnp.float32)
        rest = v - a
        b = rest.astype(jnp.bfloat16).astype(jnp.float32)
        parts = jnp.concatenate([a, b, rest - b], axis=0).astype(jnp.bfloat16)
        total = total + lax.dot_general(
            parts, hits[s, :, :], (((1,), (1,)), ((), ())), preferred_element_type=jnp.float32
        )
    summed = total[0:SUB] + total[SUB : 2 * SUB] + total[2 * SUB :]
    sens[...] = summed[0:6].reshape(6, 1, NODE_DEV)
    store.wait()

    for copy in j_copies + id_copies + val_copies + rims0 + rims1:
        copy.wait_send()
    halo_sent(*halo0)
    halo_sent(*halo1)
    halo_sent(*scales)
    halo_sent(*walls)


def hand_over(adj, sens, adj_out, sens_out, adj_v, sens_v, in_s, out_s):
    parts = [(sens, sens_v, sens_out)]
    for k in range(5):
        at = pl.ds(2 * k, 2)
        parts.append((adj.at[at], adj_v.at[at], adj_out.at[at]))
    ins = [pltpu.make_async_copy(a, v, in_s.at[k]) for k, (a, v, _) in enumerate(parts)]
    outs = [pltpu.make_async_copy(v, o, out_s.at[k]) for k, (_, v, o) in enumerate(parts)]
    for copy in ins:
        copy.start()
    for arrive, leave in zip(ins, outs):
        arrive.wait()
        leave.start()
    for copy in outs:
        copy.wait()


def body(B, passes, jac_blocks, psi_start, source, pseudo_step, dissipation, freq_volume,
         normals, face_owner, face_slot):
    _, _, planes_all, cells = jac_blocks.shape
    NJ, NK = psi_start.shape[3:]
    phase_angle = 2.0 * math.pi * ND * passes / BLADES
    R = cells // LANES
    rows = 25 * R
    pitch = -(-rows // SUB) * SUB
    faces = face_slot.shape[1]
    f32 = jnp.float32
    i16 = jnp.int16
    field, plane = (10, NJ, NK), (NJ, NK)
    hbm = pl.BlockSpec(memory_space=pl.ANY)
    vm = pl.BlockSpec(memory_space=pltpu.VMEM)
    dma = pltpu.SemaphoreType.DMA
    adj, sens = pl.pallas_call(
        functools.partial(kernel, B, passes, phase_angle),
        out_shape=(
            jax.ShapeDtypeStruct(field, f32),
            jax.ShapeDtypeStruct((6, 1, NODE_DEV), f32),
        ),
        in_specs=[hbm] * 9,
        out_specs=(hbm, vm),
        scratch_shapes=[
            pltpu.VMEM((25, planes_all, cells), jnp.bfloat16),
            pltpu.VMEM(field, f32),
            pltpu.VMEM(plane, f32),
            pltpu.VMEM(plane, f32),
            pltpu.VMEM(plane, f32),
            pltpu.VMEM((3, 1, faces), f32),
            pltpu.VMEM((1, faces), jnp.int32),
            pltpu.VMEM((1, faces), jnp.int32),
            pltpu.VMEM(field, f32),
            pltpu.VMEM((SUB, LANES), f32),
            pltpu.VMEM((SUB, LANES), jnp.int32),
            pltpu.VMEM((planes_all * pitch, LANES), f32),
            pltpu.VMEM((planes_all, rows, LANES), jnp.bfloat16),
            pltpu.VMEM((planes_all, rows, LANES), jnp.bfloat16),
            pltpu.VMEM((B * rows, LANES), f32),
            pltpu.VMEM((10, NJ + 2 * SUB, NK), f32),
            pltpu.VMEM((10, NJ + 2 * SUB, NK), f32),
            pltpu.VMEM(field, f32),
            pltpu.VMEM(field, f32),
            pltpu.VMEM(field, i16),
            pltpu.VMEM(field, i16),
            pltpu.VMEM(field, i16),
            pltpu.VMEM(field, i16),
            pltpu.VMEM(field, i16),
            pltpu.VMEM(field, i16),
            pltpu.VMEM((2 * SUB, NK), f32),
            pltpu.VMEM((2 * SUB, NK), f32),
            pltpu.VMEM((2 * SUB, NK), f32),
            pltpu.VMEM((2, 2, 2 * SUB, NK), f32),
            pltpu.VMEM((2, 2, 2 * SUB, NK), f32),
            pltpu.VMEM((B, SUB, LANES), jnp.int32),
            pltpu.VMEM((B, SUB, LANES), f32),
            pltpu.VMEM((B, NODE_DEV, LANES), jnp.bfloat16),
            pltpu.VMEM((3, NK, LANES), f32),
            pltpu.VMEM((2 * SUB, LANES), f32),
            pltpu.VMEM((2 * SUB, LANES), f32),
            pltpu.VMEM((2 * SUB, LANES), f32),
            pltpu.VMEM((2, 2 * SUB, LANES), f32),
            dma((9,)), dma,
            dma((B,)), dma((B,)),
            dma((2, 2)), dma((2, 2)),
            dma((1, 2)), dma((1, 2)),
            dma((1, 2)), dma((1, 2)),
            dma((2, 2)), dma((2, 2)),
            dma((B,)), dma((B,)),
            dma((B,)), dma((B,)),
        ],
        compiler_params=pltpu.CompilerParams(collective_id=0, has_side_effects=True),
        name="flutter",
    )(jac_blocks[0], psi_start[0, :, 0], source[0, :, 0], pseudo_step[0, 0], dissipation[0, 0],
      freq_volume[0, 0], normals[0], face_owner[:, :, 0], face_slot)
    adj, sens = pl.pallas_call(
        hand_over,
        out_shape=(
            jax.ShapeDtypeStruct(field, f32),
            jax.ShapeDtypeStruct((6, 1, NODE_DEV), f32),
        ),
        in_specs=[hbm, hbm],
        out_specs=(hbm, hbm),
        scratch_shapes=[
            pltpu.VMEM(field, f32),
            pltpu.VMEM((6, 1, NODE_DEV), f32),
            dma((6,)), dma((6,)),
        ],
        name="hand_over",
    )(adj, sens)
    return adj[None, :, None], jnp.transpose(sens, (1, 0, 2))


def solution(mesh):
    placed = (
        P("passage", None, None, "brick"),
        P("passage", None, "brick", None, None),
        P("passage", None, "brick", None, None),
        P("passage", "brick", None, None),
        P("passage", "brick", None, None),
        P("passage", "brick", None, None),
        P("passage", None, "brick", None),
        P("passage", "brick", None),
        P("passage", "brick"),
    )
    return jax.shard_map(
        functools.partial(body, mesh.shape["brick"], mesh.shape["passage"]),
        mesh=mesh,
        in_specs=placed,
        out_specs=(P("passage", None, "brick", None, None), P("passage", None, "brick")),
        check_vma=False,
    )
```

profile of v0, /device:TPU:0, one launch (start us, length us, event | category | flops | bytes accessed | tf_op | source)
XLA Modules:
  0.0 32.0 jit_solution(2119600905653804847)
XLA Ops:
  0.6 29.6 %flutter.1 = (f32[10,64,128]{2,1,0:T(8,128)}, f32[6,1,256]{2,1,0:T(1,128)}) custom-call(bf16[25,16,512]{2,1,0:T(8,128)(2,1)} %bitcast.12, f32[10,64,128]{2,1,0:T(8,128)} %bitcast.13, f32[10,64,128]{2,1,0:T(8,128)} %bitcast.14, f32[64,128]{1,0:T(8,128)} %bitcast.15, f32[64,128]{1,0:T(8,128)} %bitcast.16, f32[64,128]{1,0:T(8,128)} %bitcast.17, ...), custom_call_target="tpu_custom_call" | custom-call | tf_op jit(solution)/shard_map/flutter/pallas_call | solution.py:382
  30.3 1.7 %hand_over.1 = (f32[10,64,128]{2,1,0:T(8,128)}, f32[6,1,256]{2,1,0:T(1,128)}) custom-call(f32[10,64,128]{2,1,0:T(8,128)} %get-tuple-element.6.adj, f32[6,1,256]{2,1,0:T(1,128)} %get-tuple-element.7.sens), custom_call_target="tpu_custom_call" | custom-call | tf_op jit(solution)/shard_map/hand_over/pallas_call | solution.py:442
where the time goes:
time: 32.2 us; the launch traced here: 32 us
  Pallas kernels  31.3 us (97%)
  between operations  0.64 us (2%)
    pallas_call x1, Pallas kernels, body(): pl.pallas_call(functools.partial(kernel, B, passes, phase_angle), out_sha...  29.6 us
    pallas_call x1, Pallas kernels, body(): pl.pallas_call(hand_over, out_shape=(jax.ShapeDtypeStruct(field, f32), ja...  1.72 us

commit v1 on v0

--- a/solution.py
+++ b/solution.py
@@ -22,12 +22,12 @@
 def kernel(
     B, passes, phase_angle,
     jac_h, psi_h, source_h, pstep_h, diss_h, freq_h, normals_h, owner_h, slot_h,
-    adj_h, sens,
-    jac, source, pstep, diss, freq, normals_v, owner, slot, adj, normals, ids,
+    adj, sens,
+    jac, source, pstep, diss, freq, normals_v, owner, slot, normals, ids,
     jpack, jsend, jrecv, jflat, pad0, pad1, low, high,
     code0, low0, high0, code1, low1, high1, scale1, low_scale, high_scale,
     rim_send, rim_recv, idbuf, valbuf, hits, turned, wall_send, low_wall, high_wall, rim_wall,
-    l_s, o_s, j_s, j_r, h_s, h_r, c_s, c_r, w_s, w_r, r_s, r_r, i_s, i_r, v_s, v_r,
+    l_s, j_s, j_r, h_s, h_r, c_s, c_r, w_s, w_r, r_s, r_r, i_s, i_r, v_s, v_r,
 ):
     me = lax.axis_index("brick")
     mp = lax.axis_index("passage")
@@ -153,17 +153,24 @@
     ids[0:1, pl.ds(0, faces)] = owner[...] * NODE_DEV + slot[...]
     idbuf[pl.ds(me, 1), :, :] = ids[...].reshape(1, SUB, LANES)
 
+    def await_all(ref, sem):
+        whole = ref.at[pl.ds(0, B - 1)]
+        pltpu.make_async_copy(whole, whole, sem).wait()
+
     j_copies, id_copies, val_copies = [], [], []
-    for k, d in enumerate(others):
-        peer = lax.rem(me + d, B)
+    for k, d in enumerate(list(range(B // 2, B)) + list(range(1, B // 2))[::-1]):
+        peer = me
+        for b in range(B.bit_length() - 1):
+            if d >> b & 1:
+                peer = peer + (1 << b) * (1 - 2 * lax.rem(lax.div(me, 1 << b), 2))
         j_copies.append(pltpu.make_async_remote_copy(
-            src_ref=jsend.at[peer], dst_ref=jrecv.at[me], send_sem=j_s.at[k], recv_sem=j_r.at[k],
+            src_ref=jsend.at[peer], dst_ref=jrecv.at[me], send_sem=j_s, recv_sem=j_r,
             device_id={"brick": peer}, device_id_type=MESH))
         id_copies.append(pltpu.make_async_remote_copy(
-            src_ref=ids, dst_ref=idbuf.at[me], send_sem=i_s.at[k], recv_sem=i_r.at[k],
+            src_ref=ids, dst_ref=idbuf.at[me], send_sem=i_s, recv_sem=i_r,
             device_id={"brick": peer}, device_id_type=MESH))
         val_copies.append(pltpu.make_async_remote_copy(
-            src_ref=valbuf.at[me], dst_ref=valbuf.at[me], send_sem=v_s.at[k], recv_sem=v_r.at[k],
+            src_ref=valbuf.at[me], dst_ref=valbuf.at[me], send_sem=v_s, recv_sem=v_r,
             device_id={"brick": peer}, device_id_type=MESH))
     rims0, rims1 = rim_copies(0), rim_copies(1)
     halo0 = halo_copies(h_s, h_r, 0, code0, low0, high0)
@@ -249,8 +256,7 @@
 
     turn_over(0, [(0, 0, pstep[...]), (1, 0, diss[...]), (2, 0, freq[...])]
               + [(SUB + c + c // 5 * 3, 0, source[c, :, :]) for c in range(10)])
-    for copy in id_copies:
-        copy.wait_recv()
+    await_all(idbuf, i_r)
     node = lax.broadcasted_iota(jnp.int32, (NODE_DEV, LANES), 0) + me * NODE_DEV
     for s in range(B):
         hits[s, :, :] = jnp.where(idbuf[s, 0:1, :] == node, 1.0, 0.0).astype(jnp.bfloat16)
@@ -262,8 +268,7 @@
     for code, field in ((low0, low), (high0, high)):
         for c in range(10):
             field[c, :, :] = code[c, :, :].astype(jnp.int32).astype(jnp.float32) * (BOUND / CODE)
-    for copy in j_copies:
-        copy.wait_recv()
+    await_all(jrecv, j_r)
     for s in range(B):
         jflat[pl.ds(s * rows, rows), :] = jrecv[s, :, :].astype(jnp.float32)
 
@@ -320,12 +325,8 @@
             f = code[c, :, :].astype(jnp.int32).astype(jnp.float32)
             field[c, :, :] = f * scale[pl.ds(c, 1), :]
     advance(pad1, low, high, adj, 0)
-    store = pltpu.make_async_copy(adj, adj_h, o_s)
-
-    store.start()
-
-    for copy in val_copies:
-        copy.wait_recv()
+
+    await_all(valbuf, v_r)
     total = jnp.zeros((3 * SUB, NODE_DEV), jnp.float32)
     for s in range(B):
         v = valbuf[s, :, :]
@@ -338,9 +339,11 @@
         )
     summed = total[0:SUB] + total[SUB : 2 * SUB] + total[2 * SUB :]
     sens[...] = summed[0:6].reshape(6, 1, NODE_DEV)
-    store.wait()
-
-    for copy in j_copies + id_copies + val_copies + rims0 + rims1:
+
+    await_all(jsend, j_s)
+    await_all(idbuf, i_s)
+    await_all(valbuf, v_s)
+    for copy in rims0 + rims1:
         copy.wait_send()
     halo_sent(*halo0)
     halo_sent(*halo1)
@@ -348,18 +351,10 @@
     halo_sent(*walls)
 
 
-def hand_over(adj, sens, adj_out, sens_out, adj_v, sens_v, in_s, out_s):
-    parts = [(sens, sens_v, sens_out)]
-    for k in range(5):
-        at = pl.ds(2 * k, 2)
-        parts.append((adj.at[at], adj_v.at[at], adj_out.at[at]))
-    ins = [pltpu.make_async_copy(a, v, in_s.at[k]) for k, (a, v, _) in enumerate(parts)]
-    outs = [pltpu.make_async_copy(v, o, out_s.at[k]) for k, (_, v, o) in enumerate(parts)]
-    for copy in ins:
-        copy.start()
-    for arrive, leave in zip(ins, outs):
-        arrive.wait()
-        leave.start()
+def hand_over(adj, sens, adj_out, sens_out, out_s):
+    outs = [pltpu.make_async_copy(adj, adj_out, out_s.at[0]), pltpu.make_async_copy(sens, sens_out, out_s.at[1])]
+    for copy in outs:
+        copy.start()
     for copy in outs:
         copy.wait()
 
@@ -382,11 +377,11 @@
     adj, sens = pl.pallas_call(
         functools.partial(kernel, B, passes, phase_angle),
         out_shape=(
-            jax.ShapeDtypeStruct(field, f32),
-            jax.ShapeDtypeStruct((6, 1, NODE_DEV), f32),
+            pltpu.VMEM(field, f32),
+            pltpu.VMEM((6, 1, NODE_DEV), f32),
         ),
         in_specs=[hbm] * 9,
-        out_specs=(hbm, vm),
+        out_specs=(vm, vm),
         scratch_shapes=[
             pltpu.VMEM((25, planes_all, cells), jnp.bfloat16),
             pltpu.VMEM(field, f32),
@@ -396,7 +391,6 @@
             pltpu.VMEM((3, 1, faces), f32),
             pltpu.VMEM((1, faces), jnp.int32),
             pltpu.VMEM((1, faces), jnp.int32),
-            pltpu.VMEM(field, f32),
             pltpu.VMEM((SUB, LANES), f32),
             pltpu.VMEM((SUB, LANES), jnp.int32),
             pltpu.VMEM((planes_all * pitch, LANES), f32),
@@ -426,31 +420,31 @@
             pltpu.VMEM((2 * SUB, LANES), f32),
             pltpu.VMEM((2 * SUB, LANES), f32),
             pltpu.VMEM((2, 2 * SUB, LANES), f32),
-            dma((9,)), dma,
-            dma((B,)), dma((B,)),
+            dma((9,)),
+            dma, dma,
             dma((2, 2)), dma((2, 2)),
             dma((1, 2)), dma((1, 2)),
             dma((1, 2)), dma((1, 2)),
             dma((2, 2)), dma((2, 2)),
-            dma((B,)), dma((B,)),
-            dma((B,)), dma((B,)),
+            dma, dma,
+            dma, dma,
         ],
         compiler_params=pltpu.CompilerParams(collective_id=0, has_side_effects=True),
         name="flutter",
     )(jac_blocks[0], psi_start[0, :, 0], source[0, :, 0], pseudo_step[0, 0], dissipation[0, 0],
       freq_volume[0, 0], normals[0], face_owner[:, :, 0], face_slot)
+    adj = pltpu.with_memory_space_constraint(adj, pltpu.VMEM)
+    sens = pltpu.with_memory_space_constraint(sens, pltpu.VMEM)
     adj, sens = pl.pallas_call(
         hand_over,
         out_shape=(
             jax.ShapeDtypeStruct(field, f32),
             jax.ShapeDtypeStruct((6, 1, NODE_DEV), f32),
         ),
-        in_specs=[hbm, hbm],
+        in_specs=[vm, vm],
         out_specs=(hbm, hbm),
         scratch_shapes=[
-            pltpu.VMEM(field, f32),
-            pltpu.VMEM((6, 1, NODE_DEV), f32),
-            dma((6,)), dma((6,)),
+            dma((2,)),
         ],
         name="hand_over",
     )(adj, sens)

time: 32.2 us -> 29.6 us (0.919)
  Pallas kernels: 31.3 us -> 28.8 us
    pallas_call x1, Pallas kernels: 29.6 us -> 28 us  [body(): pl.pallas_call(functools.partial(kernel, B, passes, phase_angle), out_sha...]
    pallas_call x1, Pallas kernels: 1.72 us -> 0.75 us  [body(): pl.pallas_call(hand_over, out_shape=(jax.ShapeDtypeStruct(field, f32), ja...]
where the time goes in v1:
time: 29.6 us; the launch traced here: 29.4 us
  Pallas kernels  28.8 us (97%)
  between operations  0.64 us (2%)
    pallas_call x1, Pallas kernels, body(): pl.pallas_call(functools.partial(kernel, B, passes, phase_angle), out_sha...  28 us
    pallas_call x1, Pallas kernels, body(): pl.pallas_call(hand_over, out_shape=(jax.ShapeDtypeStruct(field, f32), ja...  0.75 us

profile of v1, /device:TPU:0, one launch (start us, length us, event | category | flops | bytes accessed | tf_op | source)
XLA Modules:
  0.0 29.4 jit_solution(9722453467067137056)
XLA Ops:
  0.6 28.0 %flutter.1 = (f32[10,64,128]{2,1,0:T(8,128)S(1)}, f32[6,1,256]{2,1,0:T(1,128)S(1)}) custom-call(bf16[25,16,512]{2,1,0:T(8,128)(2,1)} %bitcast.12, f32[10,64,128]{2,1,0:T(8,128)} %bitcast.13, f32[10,64,128]{2,1,0:T(8,128)} %bitcast.14, f32[64,128]{1,0:T(8,128)} %bitcast.15, f32[64,128]{1,0:T(8,128)} %bitcast.16, f32[64,128]{1,0:T(8,128)} %bitcast.17, ...), custom_call_target="tpu_custom_call" | custom-call | tf_op jit(solution)/shard_map/flutter/pallas_call | solution.py:377
  28.7 0.7 %hand_over.1 = (f32[10,64,128]{2,1,0:T(8,128)}, f32[6,1,256]{2,1,0:T(1,128)}) custom-call(f32[10,64,128]{2,1,0:T(8,128)S(1)} %get-tuple-element.6.adj, f32[6,1,256]{2,1,0:T(1,128)S(1)} %get-tuple-element.7.sens), custom_call_target="tpu_custom_call" | custom-call | tf_op jit(solution)/shard_map/hand_over/pallas_call | solution.py:438

commit v2 on v1

v2 whole, which is shorter than its diff:
```python
import functools
import math

import jax
import jax.numpy as jnp
from jax import lax
from jax.experimental import pallas as pl
from jax.experimental.pallas import tpu as pltpu
from jax.sharding import PartitionSpec as P

NODE_DEV = 256
SWEEPS = 2
ND = 1
BLADES = 36
LANES = 128
SUB = 8
CODE = 32767.0
BOUND = 6.0
MESH = pl.DeviceIdType.MESH


def flip(index, mask, count):
    other = index
    for b in range(count.bit_length() - 1):
        if mask >> b & 1:
            other = other + (1 << b) * (1 - 2 * lax.rem(lax.div(index, 1 << b), 2))
    return other


def kernel(
    B, passes, phase_angle,
    jac_h, psi_h, source_h, pstep_h, diss_h, freq_h, normals_h, owner_h, slot_h,
    adj, sens,
    jac, source, pstep, diss, freq, normals_v, owner, slot,
    jpack, jsend, jrecv, jflat, pad0, pad1,
    code0, low0, high0, code1, low1, high1, rim_send, rim_recv,
    mix, turned, stage, jturn, jwall, jw_send, jw_recv,
    wall, wall_low, wall_high, wall_rim, idbuf, valbuf, hits,
    l_s, j_s, j_r, jw_s, jw_r, i_s, i_r, v_s, v_r,
    h_s, h_r, g_s, g_r, w_s, w_r, r_s, r_r, q_s, q_r,
):
    me = lax.axis_index("brick")
    mp = lax.axis_index("passage")
    NJ, NK = source.shape[1], source.shape[2]
    R = jac.shape[2] // LANES
    planes = jac.shape[1]
    rows = 25 * R
    pitch = jpack.shape[0] // planes
    T = NJ // SUB
    G = SUB // R
    mine = lax.div(me, G)
    up_p = lax.rem(mp + 1, passes)
    down_p = lax.rem(mp + passes - 1, passes)
    f32 = jnp.float32

    barrier = pltpu.get_barrier_semaphore()
    for d in range(1, B):
        pl.semaphore_signal(
            barrier, inc=1, device_id={"brick": lax.rem(me + d, B)}, device_id_type=MESH
        )
    pl.semaphore_signal(barrier, inc=1, device_id={"passage": up_p}, device_id_type=MESH)
    greeted = B
    if passes > 2:
        pl.semaphore_signal(barrier, inc=1, device_id={"passage": down_p}, device_id_type=MESH)
        greeted += 1

    psi = pad0.at[:, pl.ds(SUB, NJ), :]
    loads = [
        pltpu.make_async_copy(src, dst, l_s.at[k])
        for k, (src, dst) in enumerate((
            (psi_h, psi), (jac_h, jac), (owner_h, owner), (slot_h, slot), (normals_h, normals_v),
            (source_h, source), (pstep_h, pstep), (diss_h, diss), (freq_h, freq),
        ))
    ]
    for load in loads:
        load.start()

    @pl.when(me == 0)
    def _():
        low0[...] = jnp.zeros_like(low0)
        low1[...] = jnp.zeros_like(low1)
        wall_low[...] = jnp.zeros_like(wall_low)

    @pl.when(me == B - 1)
    def _():
        high0[...] = jnp.zeros_like(high0)
        high1[...] = jnp.zeros_like(high1)
        wall_high[...] = jnp.zeros_like(wall_high)

    def copy_to(src, dst, send, recv, axis, peer):
        return pltpu.make_async_remote_copy(
            src_ref=src, dst_ref=dst, send_sem=send, recv_sem=recv,
            device_id={axis: peer}, device_id_type=MESH,
        )

    def beside_copies(src, low, high, send, recv):
        up = copy_to(src, low, send.at[0], recv[0], "brick", lax.rem(me + 1, B))
        down = copy_to(src, high, send.at[1], recv[1], "brick", lax.rem(me + B - 1, B))
        return up, down

    def beside_start(up, down):
        @pl.when(me < B - 1)
        def _():
            up.start()

        @pl.when(me > 0)
        def _():
            down.start()

    def beside_recv(up, down):
        @pl.when(me > 0)
        def _():
            up.wait_recv()

        @pl.when(me < B - 1)
        def _():
            down.wait_recv()

    def await_bytes(ref, sem):
        pltpu.make_async_copy(ref, ref, sem).wait()

    def beside_sent(ref, send):
        @pl.when(me < B - 1)
        def _():
            await_bytes(ref, send.at[0])

        @pl.when(me > 0)
        def _():
            await_bytes(ref, send.at[1])

    lanes = lax.broadcasted_iota(jnp.int32, (NJ, NK), 1)
    lane = lax.broadcasted_iota(jnp.int32, (1, LANES), 1)
    sub = lax.broadcasted_iota(jnp.int32, (SUB, NK), 0)
    lane8 = lax.broadcasted_iota(jnp.int32, (SUB, NK), 1)

    def turn_over(slot, pieces):
        halves = [jnp.zeros((NJ, NK), f32), jnp.zeros((NJ, NK), f32)]
        for to, columns, load in pieces:
            x = jnp.concatenate([load(r) for r in range(R)], axis=0) if R > 1 else load(0)
            for half, column in enumerate(columns):
                if column is not None:
                    shift = (to - column) % NK
                    y = pltpu.roll(x, shift, 1) if shift else x
                    halves[half] = jnp.where(lanes == to, y, halves[half])
        turned[slot, :, :] = jnp.concatenate(halves, axis=0).T

    def plane_rows(ref):
        return lambda r: ref[pl.ds(r, B, stride=R), :]

    def field_rows(ref, c, shift):
        return lambda r: ref[c, pl.ds(shift + r, B, stride=R), :]

    def spread(c):
        return c + c // 5 * 3

    loads[0].wait()
    for k, row in enumerate((SUB + NJ - 1, SUB)):
        for c in range(10):
            rim_send[0, k, pl.ds(c, 1), :] = pad0[c, pl.ds(row, 1), :]
    turn_over(
        0,
        [(spread(c), (0, 1), field_rows(pad0, c, SUB)) for c in range(10)]
        + [(2 * SUB + spread(c), (None, 2), field_rows(pad0, c, SUB)) for c in range(10)],
    )
    wall[0, :, :] = turned[0, 0 : 2 * SUB, :]
    for t in range(T):
        for c in range(0, 10, 2):
            at = pl.ds(SUB + t * SUB, SUB)
            x = jnp.concatenate([pad0[c, at, :], pad0[c + 1, at, :]], axis=0)
            q = jnp.round(x * (CODE / BOUND))
            code0[t, pl.ds(c * SUB, 2 * SUB), :] = q.astype(jnp.int32).astype(jnp.int16)

    for k in (2, 3, 4):
        loads[k].wait()
    faces = owner.shape[1]
    mix[...] = jnp.zeros_like(mix)
    mix[0:1, pl.ds(0, faces)] = (owner[...] * NODE_DEV + slot[...]).astype(f32)
    for d in range(3):
        mix[1 + d : 2 + d, pl.ds(0, faces)] = normals_v[d, :, :]
    stage[...] = jnp.concatenate(
        [mix[...], jnp.zeros((LANES - SUB, LANES), f32)], axis=0
    ).T
    x = [stage[pl.ds(r, B, stride=R), :] for r in range(R)]
    mix[...] = jnp.concatenate(x + x, axis=0).T[0:SUB]
    idbuf[pl.ds(me, 1), :, :] = mix[0:1, :].reshape(1, 1, LANES)

    loads[1].wait()
    for n in range(25):
        for r in range(R):
            for g in range(planes // SUB):
                x = jac[n, pl.ds(g * SUB, SUB), pl.ds(r * LANES, LANES)].astype(f32)
                jpack[pl.ds(g * SUB * pitch + r * 25 + n, SUB, stride=pitch), :] = x
    first = lax.broadcasted_iota(jnp.int32, (SUB, LANES), 0) == lane
    first = jnp.where(first, 1.0, 0.0).astype(jnp.bfloat16)
    for p in range(planes):
        x = jpack[pl.ds(p * pitch, pitch), :]
        jsend[p, :, :] = x[0:rows].astype(jnp.bfloat16)
        x = jnp.concatenate([x, jnp.zeros((LANES - pitch, LANES), f32)], axis=0)
        y = lax.dot_general(
            first, x.astype(jnp.bfloat16), (((1,), (1,)), ((), ())), preferred_element_type=f32
        )
        jw_send[p, :, :] = y[0:2]

    j_copies, jw_copies, id_copies, val_copies = [], [], [], []
    for d in list(range(B // 2, B)) + list(range(1, B // 2))[::-1]:
        peer = flip(me, d, B)
        j_copies.append(
            copy_to(jsend.at[peer], jrecv.at[me], j_s, j_r.at[mine], "brick", peer)
        )
        jw_copies.append(copy_to(jw_send.at[peer], jw_recv.at[me], jw_s, jw_r, "brick", peer))
        id_copies.append(copy_to(idbuf.at[me], idbuf.at[me], i_s, i_r, "brick", peer))
        val_copies.append(copy_to(valbuf.at[me], valbuf.at[me], v_s, v_r, "brick", peer))

    def rim_copies(sweep):
        return [
            copy_to(
                rim_send.at[sweep, k], rim_recv.at[sweep, k], r_s.at[k], r_r.at[sweep, k],
                "passage", peer,
            )
            for k, peer in ((0, up_p), (1, down_p))
        ]

    def wall_rims(sweep):
        return [
            copy_to(
                wall.at[sweep], wall_rim.at[sweep, k], q_s.at[k], q_r.at[sweep, k],
                "passage", peer,
            )
            for k, peer in ((0, up_p), (1, down_p))
        ]

    def wall_copies(sweep):
        return beside_copies(
            wall.at[sweep], wall_low.at[sweep], wall_high.at[sweep], w_s,
            (w_r.at[sweep, 0], w_r.at[sweep, 1]),
        )

    def tile_copies(t):
        return beside_copies(
            code1.at[t], low1.at[t], high1.at[t], g_s, (g_r.at[0, t], g_r.at[1, t])
        )

    rims0, rims1 = rim_copies(0), rim_copies(1)
    halo0 = beside_copies(code0, low0, high0, h_s, (h_r.at[0], h_r.at[1]))

    pl.semaphore_wait(barrier, greeted)
    for copy in wall_rims(0) + rims0:
        copy.start()
    beside_start(*wall_copies(0))
    for copy in jw_copies:
        copy.start()
    beside_start(*halo0)
    for copy in j_copies:
        copy.start()
    for copy in id_copies:
        copy.start()

    jrecv[pl.ds(me, 1), :, :] = jsend[pl.ds(me, 1), :, :]
    jw_recv[pl.ds(me, 1), :, :] = jw_send[pl.ds(me, 1), :, :]
    for load in loads[5:]:
        load.wait()
    turn_over(
        1,
        [(k, (0, 1), plane_rows(ref)) for k, ref in enumerate((pstep, diss, freq))]
        + [(SUB + spread(c), (0, 1), field_rows(source, c, 0)) for c in range(10)],
    )

    def rotated(re, im, edge, turn):
        at_edge = mp == edge
        cosine = jnp.where(at_edge, math.cos(turn), 1.0).astype(f32)
        sine = jnp.where(at_edge, math.sin(turn), 0.0).astype(f32)
        return re * cosine - im * sine, re * sine + im * cosine

    def place_rim(sweep, pad, k):
        edge, turn, row = ((0, -phase_angle, SUB - 1), (passes - 1, phase_angle, SUB + NJ))[k]
        rim = rim_recv[sweep, k, :, :]
        parts = rotated(rim[0:5], rim[5:10], edge, turn)
        for c in range(10):
            pad[c, pl.ds(row, 1), :] = parts[c // 5][c % 5 : c % 5 + 1]

    def tile_step(t, pad, low, high, sweep):
        at = pl.ds(pl.multiple_of(t * SUB, SUB), SUB)
        here = pl.ds(pl.multiple_of(t * SUB + SUB, SUB), SUB)
        after = pl.ds(pl.multiple_of(t * SUB + 2 * SUB, SUB), SUB)
        om, ds_, ps = freq[at, :], diss[at, :], pstep[at, :]
        us = [pad[c, here, :] for c in range(10)]
        sides = []
        for ref in (low, high):
            if sweep == 0:
                scale = BOUND / CODE
            else:
                scale = ref[t, pl.ds(10 * SUB, 2 * SUB), :].astype(jnp.int32).astype(f32)[0:SUB]
                scale = scale * (1.0 / (256.0 * CODE))
            side = []
            for c in range(0, 10, 2):
                x = ref[t, pl.ds(c * SUB, 2 * SUB), :].astype(jnp.int32).astype(f32)
                side += [x[0:SUB] * scale, x[SUB : 2 * SUB] * scale]
            sides.append(side)
        lows, highs = sides
        diff = [0.5 * (h - l) for h, l in zip(highs, lows)]
        conv = [None] * 10
        for n in range(5):
            for m in range(5):
                tile = jflat[t, pl.ds(n * 5 + m, SUB, stride=25), :]
                for part in (0, 5):
                    term = tile * diff[part + n]
                    conv[part + m] = term if conv[part + m] is None else conv[part + m] + term
        fresh = []
        for c in range(10):
            u = us[c]
            above = jnp.where(
                sub == SUB - 1, pltpu.roll(pad[c, after, :], SUB - 1, 0), pltpu.roll(u, SUB - 1, 0)
            )
            below = jnp.where(sub == 0, pltpu.roll(pad[c, at, :], 1, 0), pltpu.roll(u, 1, 0))
            beside = highs[c] + lows[c] + above + below
            beside = beside + jnp.where(lane8 == NK - 1, 0.0, pltpu.roll(u, NK - 1, 1))
            beside = beside + jnp.where(lane8 == 0, 0.0, pltpu.roll(u, 1, 1))
            spin = om * us[c + 5] if c < 5 else -(om * us[c - 5])
            resid = conv[c] + spin + ds_ * (6.0 * u - beside) - source[c, at, :]
            fresh.append(u - ps * resid)
        return fresh

    def first_step(u):
        t = flip(mine, u, T)
        @pl.when(t == 0)
        def _():
            rims0[0].wait_recv()
            place_rim(0, pad0, 0)

        @pl.when(t == T - 1)
        def _():
            rims0[1].wait_recv()
            place_rim(0, pad0, 1)

        count = G if u else G - 1
        if count:
            await_bytes(jrecv.at[pl.ds(0, count)], j_r.at[t])
        for g in range(G):
            jflat[t, pl.ds(g * rows, rows), :] = jrecv[t * G + g, :, :].astype(f32)
        fresh = tile_step(t, pad0, low0, high0, 0)
        here = pl.ds(pl.multiple_of(t * SUB + SUB, SUB), SUB)
        top = jnp.abs(fresh[0])
        for c in range(10):
            pad1[c, here, :] = fresh[c]
            top = jnp.maximum(top, jnp.abs(fresh[c]))
        for k, (tile, row) in enumerate(((T - 1, SUB - 1), (0, 0))):
            @pl.when(t == tile)
            def _():
                for c in range(10):
                    rim_send[1, k, pl.ds(c, 1), :] = fresh[c][row : row + 1]
                rims1[k].start()

        top = jnp.floor(jnp.max(top, axis=0, keepdims=True) * 256.0) + 1.0
        top = jnp.broadcast_to(top, (2 * SUB, NK))
        scale = (256.0 * CODE) / top
        for c in range(0, 10, 2):
            x = jnp.concatenate([fresh[c], fresh[c + 1]], axis=0)
            q = jnp.round(x * scale)
            code1[t, pl.ds(c * SUB, 2 * SUB), :] = q.astype(jnp.int32).astype(jnp.int16)
        code1[t, pl.ds(10 * SUB, 2 * SUB), :] = top.astype(jnp.int32).astype(jnp.int16)
        beside_start(*tile_copies(t))

    def second_step(t):
        @pl.when(t == 0)
        def _():
            rims1[0].wait_recv()
            place_rim(1, pad1, 0)

        @pl.when(t == T - 1)
        def _():
            rims1[1].wait_recv()
            place_rim(1, pad1, 1)

        beside_recv(*tile_copies(t))
        fresh = tile_step(t, pad1, low1, high1, 1)
        for c in range(10):
            adj[c, pl.ds(pl.multiple_of(t * SUB, SUB), SUB), :] = fresh[c]

    place = lax.rem(lane, NJ)
    turn_of = lax.div(place, B)

    def wall_step(sweep):
        u16, low16, high16 = wall[sweep, :, :], wall_low[sweep, :, :], wall_high[sweep, :, :]
        fold = (R - 1) * B - 1

        def moved(x, shift):
            shift = shift % LANES
            return pltpu.roll(x, shift, 1) if shift else x

        rims = []
        for k, (edge, turn, shift) in enumerate((
            (0, -phase_angle, 1 - NJ), (passes - 1, phase_angle, NJ - 1),
        )):
            rim = moved(wall_rim[sweep, k, :, :], shift)
            rims.append(rotated(rim[0:5], rim[SUB : SUB + 5], edge, turn))
        out = []
        for part in range(2):
            at = slice(SUB * part, SUB * part + 5)
            other = slice(SUB * (1 - part), SUB * (1 - part) + 5)
            u, lo, hi = u16[at], low16[at], high16[at]
            diff = 0.5 * (hi - lo)
            conv = jwall[0:5, :] * diff[0:1]
            for n in range(1, 5):
                conv = conv + jwall[pl.ds(5 * n, 5), :] * diff[n : n + 1]
            below = jnp.where(turn_of == 0, moved(u, -fold), moved(u, B))
            below = jnp.where(place == 0, rims[0][part], below)
            above = jnp.where(turn_of == R - 1, moved(u, fold), moved(u, -B))
            above = jnp.where(place == NJ - 1, rims[1][part], above)
            beside = hi + lo + above + below + moved(u, NJ)
            if sweep == 0:
                second = turned[0, pl.ds(2 * SUB + SUB * part, 5), :]
                beside = beside + jnp.where(lane < NJ, 0.0, second)
            spin = turned[1, 2:3, :] * u16[other]
            spin = -spin if part else spin
            resid = conv + spin + turned[1, 1:2, :] * (6.0 * u - beside)
            resid = resid - turned[1, pl.ds(SUB + SUB * part, 5), :]
            out.append(u - turned[1, 0:1, :] * resid)
        return out

    def wall_first():
        beside_recv(*wall_copies(0))
        for copy in wall_rims(0):
            copy.wait_recv()
        await_bytes(jw_recv.at[pl.ds(0, B - 1)], jw_r)
        for s in range(B):
            for k in range(2):
                stage[pl.ds(k * B + s, 1), :] = jw_recv[s, pl.ds(k, 1), :]
        jturn[...] = stage[...].T
        total = jnp.zeros((32, LANES), f32)
        for k in range(2):
            for r in range(R):
                x = jturn[pl.ds(r * 25, 32), :]
                shift = k * (NJ - B) + r * B
                x = pltpu.roll(x, shift, 1) if shift else x
                start = k * NJ + r * B
                total = jnp.where((lane >= start) & (lane < start + B), x, total)
        jwall[...] = total
        wall[1, :, :] = jnp.zeros((2 * SUB, LANES), f32)
        for part, fresh in enumerate(wall_step(0)):
            wall[1, pl.ds(SUB * part, 5), :] = fresh
        for copy in wall_rims(1):
            copy.start()
        beside_start(*wall_copies(1))

    def wall_second():
        beside_recv(*wall_copies(1))
        for copy in wall_rims(1):
            copy.wait_recv()
        sides = mix[1:4, :]
        real, imag = [fresh[1:4] * sides for fresh in wall_step(1)]
        both = jnp.where(lane < NJ, real, pltpu.roll(imag, NJ, 1))
        valbuf[pl.ds(me, 1), :, :] = both[None]
        for copy in val_copies:
            copy.start()

    def gather_hits():
        await_bytes(idbuf.at[pl.ds(0, B - 1)], i_r)
        node = lax.broadcasted_iota(jnp.int32, (NODE_DEV, LANES), 0) + me * NODE_DEV
        node = node.astype(f32)
        for s in range(B):
            hits[s, :, :] = jnp.where(idbuf[s, :, :] == node, 1.0, 0.0).astype(jnp.bfloat16)

    def sum_nodes():
        await_bytes(valbuf.at[pl.ds(0, B - 1)], v_r)
        total = jnp.zeros((3 * SUB, NODE_DEV), f32)
        for s in range(B):
            v = valbuf[s, :, :]
            v = jnp.concatenate(
                [jnp.where(lane < NJ, v, 0.0), jnp.where(lane < NJ, 0.0, v), jnp.zeros((2, LANES), f32)],
                axis=0,
            )
            a = v.astype(jnp.bfloat16).astype(f32)
            rest = v - a
            b = rest.astype(jnp.bfloat16).astype(f32)
            parts = jnp.concatenate([a, b, rest - b], axis=0).astype(jnp.bfloat16)
            total = total + lax.dot_general(
                parts, hits[s, :, :], (((1,), (1,)), ((), ())), preferred_element_type=f32
            )
        summed = total[0:SUB] + total[SUB : 2 * SUB] + total[2 * SUB :]
        sens[...] = summed[0:6].reshape(6, 1, NODE_DEV)

    half = T // 2
    upper = lax.div(mine, half)

    def second_order(i):
        near = half - 1 - i + upper * (1 + 2 * i)
        far = half + i - upper * (1 + 2 * i)
        return near, far

    wall_first()
    beside_recv(*halo0)
    for u in range(half):
        first_step(u)
    first_step(half)
    wall_second()
    for u in range(half + 1, T):
        first_step(u)
    for side in range(2):
        for i in range(half - 1):
            second_step(second_order(i)[side])
    gather_hits()
    sum_nodes()
    for side in range(2):
        second_step(second_order(half - 1)[side])
    await_bytes(jsend.at[pl.ds(0, B - 1)], j_s)
    await_bytes(jw_send.at[pl.ds(0, B - 1)], jw_s)
    await_bytes(idbuf.at[pl.ds(0, B - 1)], i_s)
    await_bytes(valbuf.at[pl.ds(0, B - 1)], v_s)
    for k in range(2):
        await_bytes(rim_send.at[k], r_s.at[k])
        await_bytes(wall, q_s.at[k])
    beside_sent(code0, h_s)
    beside_sent(code1, g_s)
    beside_sent(wall, w_s)


def hand_over(adj, sens, adj_out, sens_out, out_s):
    outs = [pltpu.make_async_copy(adj, adj_out, out_s.at[0]), pltpu.make_async_copy(sens, sens_out, out_s.at[1])]
    for copy in outs:
        copy.start()
    for copy in outs:
        copy.wait()


def body(B, passes, jac_blocks, psi_start, source, pseudo_step, dissipation, freq_volume,
         normals, face_owner, face_slot):
    _, _, planes_all, cells = jac_blocks.shape
    NJ, NK = psi_start.shape[3:]
    phase_angle = 2.0 * math.pi * ND * passes / BLADES
    R = cells // LANES
    rows = 25 * R
    pitch = -(-rows // SUB) * SUB
    faces = face_slot.shape[1]
    T = NJ // SUB
    f32 = jnp.float32
    i16 = jnp.int16
    bf16 = jnp.bfloat16
    field, plane = (10, NJ, NK), (NJ, NK)
    coded, scaled = (T, 10 * SUB, NK), (T, 12 * SUB, NK)
    hbm = pl.BlockSpec(memory_space=pl.ANY)
    vm = pl.BlockSpec(memory_space=pltpu.VMEM)
    dma = pltpu.SemaphoreType.DMA
    adj, sens = pl.pallas_call(
        functools.partial(kernel, B, passes, phase_angle),
        out_shape=(
            pltpu.VMEM(field, f32),
            pltpu.VMEM((6, 1, NODE_DEV), f32),
        ),
        in_specs=[hbm] * 9,
        out_specs=(vm, vm),
        scratch_shapes=[
            pltpu.VMEM((25, planes_all, cells), bf16),
            pltpu.VMEM(field, f32),
            pltpu.VMEM(plane, f32),
            pltpu.VMEM(plane, f32),
            pltpu.VMEM(plane, f32),
            pltpu.VMEM((3, 1, faces), f32),
            pltpu.VMEM((1, faces), jnp.int32),
            pltpu.VMEM((1, faces), jnp.int32),
            pltpu.VMEM((planes_all * pitch, LANES), f32),
            pltpu.VMEM((planes_all, rows, LANES), bf16),
            pltpu.VMEM((planes_all, rows, LANES), bf16),
            pltpu.VMEM((T, 25 * SUB, LANES), f32),
            pltpu.VMEM((10, NJ + 2 * SUB, NK), f32),
            pltpu.VMEM((10, NJ + 2 * SUB, NK), f32),
            pltpu.VMEM(coded, i16),
            pltpu.VMEM(coded, i16),
            pltpu.VMEM(coded, i16),
            pltpu.VMEM(scaled, i16),
            pltpu.VMEM(scaled, i16),
            pltpu.VMEM(scaled, i16),
            pltpu.VMEM((2, 2, 2 * SUB, NK), f32),
            pltpu.VMEM((2, 2, 2 * SUB, NK), f32),
            pltpu.VMEM((SUB, LANES), f32),
            pltpu.VMEM((2, LANES, LANES), f32),
            pltpu.VMEM((LANES, LANES), f32),
            pltpu.VMEM((LANES, LANES), f32),
            pltpu.VMEM((32, LANES), f32),
            pltpu.VMEM((planes_all, 2, LANES), f32),
            pltpu.VMEM((planes_all, 2, LANES), f32),
            pltpu.VMEM((2, 2 * SUB, LANES), f32),
            pltpu.VMEM((2, 2 * SUB, LANES), f32),
            pltpu.VMEM((2, 2 * SUB, LANES), f32),
            pltpu.VMEM((2, 2, 2 * SUB, LANES), f32),
            pltpu.VMEM((B, 1, LANES), f32),
            pltpu.VMEM((B, 3, LANES), f32),
            pltpu.VMEM((B, NODE_DEV, LANES), bf16),
            dma((9,)),
            dma, dma((T,)),
            dma, dma,
            dma, dma,
            dma, dma,
            dma((2,)), dma((2,)),
            dma((2,)), dma((2, T)),
            dma((2,)), dma((2, 2)),
            dma((2,)), dma((2, 2)),
            dma((2,)), dma((2, 2)),
        ],
        compiler_params=pltpu.CompilerParams(collective_id=0, has_side_effects=True),
        name="flutter",
    )(jac_blocks[0], psi_start[0, :, 0], source[0, :, 0], pseudo_step[0, 0], dissipation[0, 0],
      freq_volume[0, 0], normals[0], face_owner[:, :, 0], face_slot)
    adj = pltpu.with_memory_space_constraint(adj, pltpu.VMEM)
    sens = pltpu.with_memory_space_constraint(sens, pltpu.VMEM)
    adj, sens = pl.pallas_call(
        hand_over,
        out_shape=(
            jax.ShapeDtypeStruct(field, f32),
            jax.ShapeDtypeStruct((6, 1, NODE_DEV), f32),
        ),
        in_specs=[vm, vm],
        out_specs=(hbm, hbm),
        scratch_shapes=[
            dma((2,)),
        ],
        name="hand_over",
    )(adj, sens)
    return adj[None, :, None], jnp.transpose(sens, (1, 0, 2))


def solution(mesh):
    placed = (
        P("passage", None, None, "brick"),
        P("passage", None, "brick", None, None),
        P("passage", None, "brick", None, None),
        P("passage", "brick", None, None),
        P("passage", "brick", None, None),
        P("passage", "brick", None, None),
        P("passage", None, "brick", None),
        P("passage", "brick", None),
        P("passage", "brick"),
    )
    return jax.shard_map(
        functools.partial(body, mesh.shape["brick"], mesh.shape["passage"]),
        mesh=mesh,
        in_specs=placed,
        out_specs=(P("passage", None, "brick", None, None), P("passage", None, "brick")),
        check_vma=False,
    )
```

time: 29.6 us -> 25.3 us (0.85)
  Pallas kernels: 28.8 us -> 24.5 us
    pallas_call x1, Pallas kernels: 28 us -> 23.8 us  [body(): pl.pallas_call(functools.partial(kernel, B, passes, phase_angle), out_sha...]
where the time goes in v2:
time: 25.3 us; the launch traced here: 25.2 us
  Pallas kernels  24.5 us (97%)
  between operations  0.64 us (3%)
    pallas_call x1, Pallas kernels, body(): pl.pallas_call(functools.partial(kernel, B, passes, phase_angle), out_sha...  23.8 us
    pallas_call x1, Pallas kernels, body(): pl.pallas_call(hand_over, out_shape=(jax.ShapeDtypeStruct(field, f32), ja...  0.75 us

profile of v2, /device:TPU:0, one launch (start us, length us, event | category | flops | bytes accessed | tf_op | source)
XLA Modules:
  0.0 25.2 jit_solution(1512422640445749563)
XLA Ops:
  0.6 23.8 %flutter.1 = (f32[10,64,128]{2,1,0:T(8,128)S(1)}, f32[6,1,256]{2,1,0:T(1,128)S(1)}) custom-call(bf16[25,16,512]{2,1,0:T(8,128)(2,1)} %bitcast.12, f32[10,64,128]{2,1,0:T(8,128)} %bitcast.13, f32[10,64,128]{2,1,0:T(8,128)} %bitcast.14, f32[64,128]{1,0:T(8,128)} %bitcast.15, f32[64,128]{1,0:T(8,128)} %bitcast.16, f32[64,128]{1,0:T(8,128)} %bitcast.17, ...), custom_call_target="tpu_custom_call" | custom-call | tf_op jit(solution)/shard_map/flutter/pallas_call | solution.py:543
  24.4 0.7 %hand_over.1 = (f32[10,64,128]{2,1,0:T(8,128)}, f32[6,1,256]{2,1,0:T(1,128)}) custom-call(f32[10,64,128]{2,1,0:T(8,128)S(1)} %get-tuple-element.6.adj, f32[6,1,256]{2,1,0:T(1,128)S(1)} %get-tuple-element.7.sens), custom_call_target="tpu_custom_call" | custom-call | tf_op jit(solution)/shard_map/hand_over/pallas_call | solution.py:605

commit v3 on v2

--- a/solution.py
+++ b/solution.py
@@ -170,20 +170,6 @@
             q = jnp.round(x * (CODE / BOUND))
             code0[t, pl.ds(c * SUB, 2 * SUB), :] = q.astype(jnp.int32).astype(jnp.int16)
 
-    for k in (2, 3, 4):
-        loads[k].wait()
-    faces = owner.shape[1]
-    mix[...] = jnp.zeros_like(mix)
-    mix[0:1, pl.ds(0, faces)] = (owner[...] * NODE_DEV + slot[...]).astype(f32)
-    for d in range(3):
-        mix[1 + d : 2 + d, pl.ds(0, faces)] = normals_v[d, :, :]
-    stage[...] = jnp.concatenate(
-        [mix[...], jnp.zeros((LANES - SUB, LANES), f32)], axis=0
-    ).T
-    x = [stage[pl.ds(r, B, stride=R), :] for r in range(R)]
-    mix[...] = jnp.concatenate(x + x, axis=0).T[0:SUB]
-    idbuf[pl.ds(me, 1), :, :] = mix[0:1, :].reshape(1, 1, LANES)
-
     loads[1].wait()
     for n in range(25):
         for r in range(R):
@@ -241,7 +227,36 @@
         )
 
     rims0, rims1 = rim_copies(0), rim_copies(1)
-    halo0 = beside_copies(code0, low0, high0, h_s, (h_r.at[0], h_r.at[1]))
+    half = T // 2
+    upper = lax.div(mine, half)
+
+    def side_of(brick):
+        return lax.div(lax.div(brick, G), half)
+
+    def halo_copies(k):
+        copies = []
+        for step, dst in ((1, low0), (B - 1, high0)):
+            peer = lax.rem(me + step, B)
+            side = side_of(peer)
+            part = side if k == 0 else 1 - side
+            at = pl.ds(part * half, half)
+            copies.append(copy_to(
+                code0.at[at], dst.at[at], h_s.at[0 if step == 1 else 1],
+                h_r.at[0 if step == 1 else 1, k], "brick", peer,
+            ))
+        return copies
+
+    def halo_recv(k):
+        part = upper if k == 0 else 1 - upper
+        at = pl.ds(part * half, half)
+
+        @pl.when(me > 0)
+        def _():
+            await_bytes(low0.at[at], h_r.at[0, k])
+
+        @pl.when(me < B - 1)
+        def _():
+            await_bytes(high0.at[at], h_r.at[1, k])
 
     pl.semaphore_wait(barrier, greeted)
     for copy in wall_rims(0) + rims0:
@@ -249,10 +264,11 @@
     beside_start(*wall_copies(0))
     for copy in jw_copies:
         copy.start()
-    beside_start(*halo0)
-    for copy in j_copies:
+    beside_start(*halo_copies(0))
+    for copy in j_copies[:B // 4]:
         copy.start()
-    for copy in id_copies:
+    beside_start(*halo_copies(1))
+    for copy in j_copies[B // 2 :]:
         copy.start()
 
     jrecv[pl.ds(me, 1), :, :] = jsend[pl.ds(me, 1), :, :]
@@ -264,6 +280,22 @@
         [(k, (0, 1), plane_rows(ref)) for k, ref in enumerate((pstep, diss, freq))]
         + [(SUB + spread(c), (0, 1), field_rows(source, c, 0)) for c in range(10)],
     )
+
+    for k in (2, 3, 4):
+        loads[k].wait()
+    faces = owner.shape[1]
+    mix[...] = jnp.zeros_like(mix)
+    mix[0:1, pl.ds(0, faces)] = (owner[...] * NODE_DEV + slot[...]).astype(f32)
+    for d in range(3):
+        mix[1 + d : 2 + d, pl.ds(0, faces)] = normals_v[d, :, :]
+    stage[...] = jnp.concatenate(
+        [mix[...], jnp.zeros((LANES - SUB, LANES), f32)], axis=0
+    ).T
+    x = [stage[pl.ds(r, B, stride=R), :] for r in range(R)]
+    mix[...] = jnp.concatenate(x + x, axis=0).T[0:SUB]
+    idbuf[pl.ds(me, 1), :, :] = mix[0:1, :].reshape(1, 1, LANES)
+    for copy in id_copies:
+        copy.start()
 
     def rotated(re, im, edge, turn):
         at_edge = mp == edge
@@ -479,29 +511,44 @@
         summed = total[0:SUB] + total[SUB : 2 * SUB] + total[2 * SUB :]
         sens[...] = summed[0:6].reshape(6, 1, NODE_DEV)
 
-    half = T // 2
-    upper = lax.div(mine, half)
-
-    def second_order(i):
-        near = half - 1 - i + upper * (1 + 2 * i)
-        far = half + i - upper * (1 + 2 * i)
-        return near, far
+    spot = lax.rem(mine, half)
+
+    def differ(p, q):
+        out = 0
+        for b in range(half.bit_length() - 1):
+            one = lax.rem(lax.div(p, 1 << b) + lax.div(q, 1 << b), 2)
+            out = out + (1 << b) * one
+        return out
+
+    def near_tile(i):
+        return half - 1 - i + upper * (1 + 2 * i)
+
+    def far_tile(i):
+        outer = (1 - upper) * (half - 1)
+        turn = differ(spot, outer)
+        if i < half - 1:
+            turn = i + lax.div(i + half - turn, half)
+        return (1 - upper) * half + differ(spot, turn)
 
     wall_first()
-    beside_recv(*halo0)
+    for copy in j_copies[B // 4 : B // 2]:
+        copy.start()
+    halo_recv(0)
     for u in range(half):
         first_step(u)
+    wall_second()
+    halo_recv(1)
     first_step(half)
-    wall_second()
     for u in range(half + 1, T):
         first_step(u)
-    for side in range(2):
-        for i in range(half - 1):
-            second_step(second_order(i)[side])
+    for i in range(half - 1):
+        second_step(near_tile(i))
     gather_hits()
+    for i in range(half - 1):
+        second_step(far_tile(i))
+    second_step(near_tile(half - 1))
+    second_step(far_tile(half - 1))
     sum_nodes()
-    for side in range(2):
-        second_step(second_order(half - 1)[side])
     await_bytes(jsend.at[pl.ds(0, B - 1)], j_s)
     await_bytes(jw_send.at[pl.ds(0, B - 1)], jw_s)
     await_bytes(idbuf.at[pl.ds(0, B - 1)], i_s)
@@ -590,7 +637,7 @@
             dma, dma,
             dma, dma,
             dma, dma,
-            dma((2,)), dma((2,)),
+            dma((2,)), dma((2, 2)),
             dma((2,)), dma((2, T)),
             dma((2,)), dma((2, 2)),
             dma((2,)), dma((2, 2)),

time: 25.3 us -> 24.1 us (0.953)
  Pallas kernels: 24.5 us -> 23.3 us
    pallas_call x1, Pallas kernels: 23.8 us -> 22.5 us  [body(): pl.pallas_call(functools.partial(kernel, B, passes, phase_angle), out_sha...]
where the time goes in v3:
time: 24.1 us; the launch traced here: 23.9 us
  Pallas kernels  23.3 us (97%)
  between operations  0.64 us (3%)
    pallas_call x1, Pallas kernels, body(): pl.pallas_call(functools.partial(kernel, B, passes, phase_angle), out_sha...  22.5 us
    pallas_call x1, Pallas kernels, body(): pl.pallas_call(hand_over, out_shape=(jax.ShapeDtypeStruct(field, f32), ja...  0.75 us

profile of v3, /device:TPU:0, one launch (start us, length us, event | category | flops | bytes accessed | tf_op | source)
XLA Modules:
  0.0 23.9 jit_solution(9285801979083144917)
XLA Ops:
  0.6 22.5 %flutter.1 = (f32[10,64,128]{2,1,0:T(8,128)S(1)}, f32[6,1,256]{2,1,0:T(1,128)S(1)}) custom-call(bf16[25,16,512]{2,1,0:T(8,128)(2,1)} %bitcast.12, f32[10,64,128]{2,1,0:T(8,128)} %bitcast.13, f32[10,64,128]{2,1,0:T(8,128)} %bitcast.14, f32[64,128]{1,0:T(8,128)} %bitcast.15, f32[64,128]{1,0:T(8,128)} %bitcast.16, f32[64,128]{1,0:T(8,128)} %bitcast.17, ...), custom_call_target="tpu_custom_call" | custom-call | tf_op jit(solution)/shard_map/flutter/pallas_call | solution.py:590
  23.2 0.7 %hand_over.1 = (f32[10,64,128]{2,1,0:T(8,128)}, f32[6,1,256]{2,1,0:T(1,128)}) custom-call(f32[10,64,128]{2,1,0:T(8,128)S(1)} %get-tuple-element.6.adj, f32[6,1,256]{2,1,0:T(1,128)S(1)} %get-tuple-element.7.sens), custom_call_target="tpu_custom_call" | custom-call | tf_op jit(solution)/shard_map/hand_over/pallas_call | solution.py:652

commit v4 on v3

--- a/solution.py
+++ b/solution.py
@@ -195,7 +195,12 @@
         )
         jw_copies.append(copy_to(jw_send.at[peer], jw_recv.at[me], jw_s, jw_r, "brick", peer))
         id_copies.append(copy_to(idbuf.at[me], idbuf.at[me], i_s, i_r, "brick", peer))
-        val_copies.append(copy_to(valbuf.at[me], valbuf.at[me], v_s, v_r, "brick", peer))
+        val_copies.append([
+            copy_to(valbuf.at[me], valbuf.at[me], v_s, v_r.at[k], "brick", peer) for k in range(2)
+        ])
+
+    centres = (B // 2 - 1, B // 2)
+    central = jnp.logical_or(me == centres[0], me == centres[1])
 
     def rim_copies(sweep):
         return [
@@ -321,7 +326,7 @@
             if sweep == 0:
                 scale = BOUND / CODE
             else:
-                scale = ref[t, pl.ds(10 * SUB, 2 * SUB), :].astype(jnp.int32).astype(f32)[0:SUB]
+                scale = ref[t, pl.ds(10 * SUB, 2), :].astype(jnp.int32).astype(f32)[0:1]
                 scale = scale * (1.0 / (256.0 * CODE))
             side = []
             for c in range(0, 10, 2):
@@ -389,7 +394,7 @@
             x = jnp.concatenate([fresh[c], fresh[c + 1]], axis=0)
             q = jnp.round(x * scale)
             code1[t, pl.ds(c * SUB, 2 * SUB), :] = q.astype(jnp.int32).astype(jnp.int16)
-        code1[t, pl.ds(10 * SUB, 2 * SUB), :] = top.astype(jnp.int32).astype(jnp.int16)
+        code1[t, pl.ds(10 * SUB, 2), :] = top[0:2].astype(jnp.int32).astype(jnp.int16)
         beside_start(*tile_copies(t))
 
     def second_step(t):
@@ -482,8 +487,16 @@
         real, imag = [fresh[1:4] * sides for fresh in wall_step(1)]
         both = jnp.where(lane < NJ, real, pltpu.roll(imag, NJ, 1))
         valbuf[pl.ds(me, 1), :, :] = both[None]
-        for copy in val_copies:
-            copy.start()
+
+        @pl.when(central)
+        def _():
+            for copies in val_copies:
+                copies[1].start()
+
+        @pl.when(jnp.logical_not(central))
+        def _():
+            for copies in val_copies:
+                copies[0].start()
 
     def gather_hits():
         await_bytes(idbuf.at[pl.ds(0, B - 1)], i_r)
@@ -492,10 +505,16 @@
         for s in range(B):
             hits[s, :, :] = jnp.where(idbuf[s, :, :] == node, 1.0, 0.0).astype(jnp.bfloat16)
 
-    def sum_nodes():
-        await_bytes(valbuf.at[pl.ds(0, B - 1)], v_r)
-        total = jnp.zeros((3 * SUB, NODE_DEV), f32)
-        for s in range(B):
+    def sum_nodes(late, total):
+        @pl.when(central)
+        def _():
+            await_bytes(valbuf.at[pl.ds(0, 1 if late else B - 2)], v_r.at[late])
+
+        @pl.when(jnp.logical_not(central))
+        def _():
+            await_bytes(valbuf.at[pl.ds(0, 2 if late else B - 3)], v_r.at[late])
+
+        for s in centres if late else [s for s in range(B) if s not in centres]:
             v = valbuf[s, :, :]
             v = jnp.concatenate(
                 [jnp.where(lane < NJ, v, 0.0), jnp.where(lane < NJ, 0.0, v), jnp.zeros((2, LANES), f32)],
@@ -508,8 +527,7 @@
             total = total + lax.dot_general(
                 parts, hits[s, :, :], (((1,), (1,)), ((), ())), preferred_element_type=f32
             )
-        summed = total[0:SUB] + total[SUB : 2 * SUB] + total[2 * SUB :]
-        sens[...] = summed[0:6].reshape(6, 1, NODE_DEV)
+        return total
 
     spot = lax.rem(mine, half)
 
@@ -541,14 +559,17 @@
     first_step(half)
     for u in range(half + 1, T):
         first_step(u)
+    gather_hits()
+    total = sum_nodes(0, jnp.zeros((3 * SUB, NODE_DEV), f32))
     for i in range(half - 1):
         second_step(near_tile(i))
-    gather_hits()
     for i in range(half - 1):
         second_step(far_tile(i))
     second_step(near_tile(half - 1))
     second_step(far_tile(half - 1))
-    sum_nodes()
+    total = sum_nodes(1, total)
+    summed = total[0:SUB] + total[SUB : 2 * SUB] + total[2 * SUB :]
+    sens[...] = summed[0:6].reshape(6, 1, NODE_DEV)
     await_bytes(jsend.at[pl.ds(0, B - 1)], j_s)
     await_bytes(jw_send.at[pl.ds(0, B - 1)], jw_s)
     await_bytes(idbuf.at[pl.ds(0, B - 1)], i_s)
@@ -583,7 +604,7 @@
     i16 = jnp.int16
     bf16 = jnp.bfloat16
     field, plane = (10, NJ, NK), (NJ, NK)
-    coded, scaled = (T, 10 * SUB, NK), (T, 12 * SUB, NK)
+    coded, scaled = (T, 10 * SUB, NK), (T, 10 * SUB + 2, NK)
     hbm = pl.BlockSpec(memory_space=pl.ANY)
     vm = pl.BlockSpec(memory_space=pltpu.VMEM)
     dma = pltpu.SemaphoreType.DMA
@@ -636,7 +657,7 @@
             dma, dma((T,)),
             dma, dma,
             dma, dma,
-            dma, dma,
+            dma, dma((2,)),
             dma((2,)), dma((2, 2)),
             dma((2,)), dma((2, T)),
             dma((2,)), dma((2, 2)),

time: 24.1 us -> 23.8 us (0.988)
  Pallas kernels: 23.3 us -> 23 us
    pallas_call x1, Pallas kernels: 22.5 us -> 22.2 us  [body(): pl.pallas_call(functools.partial(kernel, B, passes, phase_angle), out_sha...]
where the time goes in v4:
time: 23.8 us; the launch traced here: 23.6 us
  Pallas kernels  23 us (97%)
  between operations  0.64 us (3%)
    pallas_call x1, Pallas kernels, body(): pl.pallas_call(functools.partial(kernel, B, passes, phase_angle), out_sha...  22.2 us
    pallas_call x1, Pallas kernels, body(): pl.pallas_call(hand_over, out_shape=(jax.ShapeDtypeStruct(field, f32), ja...  0.75 us

profile of v4, /device:TPU:0, one launch (start us, length us, event | category | flops | bytes accessed | tf_op | source)
XLA Modules:
  0.0 23.6 jit_solution(17193095444229067924)
XLA Ops:
  0.6 22.2 %flutter.1 = (f32[10,64,128]{2,1,0:T(8,128)S(1)}, f32[6,1,256]{2,1,0:T(1,128)S(1)}) custom-call(bf16[25,16,512]{2,1,0:T(8,128)(2,1)} %bitcast.12, f32[10,64,128]{2,1,0:T(8,128)} %bitcast.13, f32[10,64,128]{2,1,0:T(8,128)} %bitcast.14, f32[64,128]{1,0:T(8,128)} %bitcast.15, f32[64,128]{1,0:T(8,128)} %bitcast.16, f32[64,128]{1,0:T(8,128)} %bitcast.17, ...), custom_call_target="tpu_custom_call" | custom-call | tf_op jit(solution)/shard_map/flutter/pallas_call | solution.py:611
  22.9 0.7 %hand_over.1 = (f32[10,64,128]{2,1,0:T(8,128)}, f32[6,1,256]{2,1,0:T(1,128)}) custom-call(f32[10,64,128]{2,1,0:T(8,128)S(1)} %get-tuple-element.6.adj, f32[6,1,256]{2,1,0:T(1,128)S(1)} %get-tuple-element.7.sens), custom_call_target="tpu_custom_call" | custom-call | tf_op jit(solution)/shard_map/hand_over/pallas_call | solution.py:673

commit v5 on v4

--- a/solution.py
+++ b/solution.py
@@ -270,11 +270,9 @@
     for copy in jw_copies:
         copy.start()
     beside_start(*halo_copies(0))
-    for copy in j_copies[:B // 4]:
+    for copy in j_copies[: B // 8] + j_copies[B // 2 :] + j_copies[B // 8 : B // 4]:
         copy.start()
     beside_start(*halo_copies(1))
-    for copy in j_copies[B // 2 :]:
-        copy.start()
 
     jrecv[pl.ds(me, 1), :, :] = jsend[pl.ds(me, 1), :, :]
     jw_recv[pl.ds(me, 1), :, :] = jw_send[pl.ds(me, 1), :, :]

time: 23.8 us -> 23.5 us (0.987)
  Pallas kernels: 23 us -> 22.7 us
    pallas_call x1, Pallas kernels: 22.2 us -> 22 us  [body(): pl.pallas_call(functools.partial(kernel, B, passes, phase_angle), out_sha...]
where the time goes in v5:
time: 23.5 us; the launch traced here: 23.4 us
  Pallas kernels  22.7 us (97%)
  between operations  0.64 us (3%)
    pallas_call x1, Pallas kernels, body(): pl.pallas_call(functools.partial(kernel, B, passes, phase_angle), out_sha...  22 us
    pallas_call x1, Pallas kernels, body(): pl.pallas_call(hand_over, out_shape=(jax.ShapeDtypeStruct(field, f32), ja...  0.75 us

profile of v5, /device:TPU:0, one launch (start us, length us, event | category | flops | bytes accessed | tf_op | source)
XLA Modules:
  0.0 23.4 jit_solution(12584714586761159046)
XLA Ops:
  0.6 22.0 %flutter.1 = (f32[10,64,128]{2,1,0:T(8,128)S(1)}, f32[6,1,256]{2,1,0:T(1,128)S(1)}) custom-call(bf16[25,16,512]{2,1,0:T(8,128)(2,1)} %bitcast.12, f32[10,64,128]{2,1,0:T(8,128)} %bitcast.13, f32[10,64,128]{2,1,0:T(8,128)} %bitcast.14, f32[64,128]{1,0:T(8,128)} %bitcast.15, f32[64,128]{1,0:T(8,128)} %bitcast.16, f32[64,128]{1,0:T(8,128)} %bitcast.17, ...), custom_call_target="tpu_custom_call" | custom-call | tf_op jit(solution)/shard_map/flutter/pallas_call | solution.py:609
  22.6 0.7 %hand_over.1 = (f32[10,64,128]{2,1,0:T(8,128)}, f32[6,1,256]{2,1,0:T(1,128)}) custom-call(f32[10,64,128]{2,1,0:T(8,128)S(1)} %get-tuple-element.6.adj, f32[6,1,256]{2,1,0:T(1,128)S(1)} %get-tuple-element.7.sens), custom_call_target="tpu_custom_call" | custom-call | tf_op jit(solution)/shard_map/hand_over/pallas_call | solution.py:671

commit v6 on v5

--- a/solution.py
+++ b/solution.py
@@ -270,7 +270,7 @@
     for copy in jw_copies:
         copy.start()
     beside_start(*halo_copies(0))
-    for copy in j_copies[: B // 8] + j_copies[B // 2 :] + j_copies[B // 8 : B // 4]:
+    for copy in j_copies[: B // 8] + j_copies[B // 2 :] + j_copies[B // 8 : 3 * B // 16]:
         copy.start()
     beside_start(*halo_copies(1))
 
@@ -547,7 +547,7 @@
         return (1 - upper) * half + differ(spot, turn)
 
     wall_first()
-    for copy in j_copies[B // 4 : B // 2]:
+    for copy in j_copies[3 * B // 16 : B // 2]:
         copy.start()
     halo_recv(0)
     for u in range(half):

time: 23.5 us -> 23.5 us (level)
  the two profiles are of different devices: /device:TPU:0 before, /device:TPU:13 now
where the time goes in v6:
time: 23.5 us; the launch traced here: 23.4 us
  Pallas kernels  22.7 us (97%)
  between operations  0.64 us (3%)
    pallas_call x1, Pallas kernels, body(): pl.pallas_call(functools.partial(kernel, B, passes, phase_angle), out_sha...  22 us
    pallas_call x1, Pallas kernels, body(): pl.pallas_call(hand_over, out_shape=(jax.ShapeDtypeStruct(field, f32), ja...  0.75 us

profile of v6, /device:TPU:13, one launch (start us, length us, event | category | flops | bytes accessed | tf_op | source)
XLA Modules:
  0.0 23.4 jit_solution(5856062033064897244)
XLA Ops:
  0.6 22.0 %flutter.1 = (f32[10,64,128]{2,1,0:T(8,128)S(1)}, f32[6,1,256]{2,1,0:T(1,128)S(1)}) custom-call(bf16[25,16,512]{2,1,0:T(8,128)(2,1)} %bitcast.12, f32[10,64,128]{2,1,0:T(8,128)} %bitcast.13, f32[10,64,128]{2,1,0:T(8,128)} %bitcast.14, f32[64,128]{1,0:T(8,128)} %bitcast.15, f32[64,128]{1,0:T(8,128)} %bitcast.16, f32[64,128]{1,0:T(8,128)} %bitcast.17, ...), custom_call_target="tpu_custom_call" | custom-call | tf_op jit(solution)/shard_map/flutter/pallas_call | solution.py:609
  22.6 0.7 %hand_over.1 = (f32[10,64,128]{2,1,0:T(8,128)}, f32[6,1,256]{2,1,0:T(1,128)}) custom-call(f32[10,64,128]{2,1,0:T(8,128)S(1)} %get-tuple-element.6.adj, f32[6,1,256]{2,1,0:T(1,128)S(1)} %get-tuple-element.7.sens), custom_call_target="tpu_custom_call" | custom-call | tf_op jit(solution)/shard_map/hand_over/pallas_call | solution.py:671
